TPU v7x, 32 devices: a whole 2x2x4 slice. The times are simulated.
32 devices in a mesh: row: 4 (over z), col: 8 (over y, x, core).
Axes of the slice: x: 2, y: 2, z: 4, core: 2. Of those that a mesh axis runs over, the one named last changes fastest.
Arguments:
- charges: bfloat16 [64, 48, 1024], P(('row', 'col')), may hold values from -6 to 6
- near_blocks: bfloat16 [64, 2, 1024, 1024], P(('row', 'col')), may hold values from -0.125 to 0.125
- near_src: int32 [64, 2], P(('row', 'col')), may hold values from 0 to 63, as said below
- far_v: bfloat16 [32, 32, 4, 32, 1024], P(('row', 'col')), may hold values from -0.1875 to 0.1875
- far_u: bfloat16 [32, 32, 4, 32, 1024], P(('row', 'col')), may hold values from -0.125 to 0.125
- far_rank: int32 [32, 32, 4], P(('row', 'col')), may hold values from 0 to 32, as said below
- far_col: int32 [32, 32, 4], P(('row', 'col')), may hold values from 0 to 1
- far_row: int32 [32, 32, 4], P(('row', 'col')), may hold values from 0 to 1
Outputs:
- potential: float32 [64, 48, 1024], P(('row', 'col'))
Inputs may be any that keep to these rules, and one draw needn't show every extreme that they name: near_src[i, n] is a cluster of a device with the same row index as cluster i's device, whose col index differs from it by at most one, cyclically over 8. `far_rank`: in every draw some device receives only used slots (rank above 0) from every device.
All inputs are finite; a program needn't handle non-finite values.
Results may differ from a plain program's by a relative error of at most 0.0017.
Values may be sent and summed in bfloat16 or wider, within the bound.
A program may use at most 128 MiB of HBM per device.

v0:
```python
import jax
import jax.numpy as jnp
from jax import lax
from jax.sharding import PartitionSpec as P


def with_halo(x, sides, width):
    for axis, dim in sides:
        devices, length = (lax.axis_size(axis), x.shape[dim])
        up = [(i, (i + 1) % devices) for i in range(devices)]
        down = [(j, i) for i, j in up]
        last = lax.slice_in_dim(x, length - width, length, axis=dim)
        first = lax.slice_in_dim(x, 0, width, axis=dim)
        before = lax.ppermute(last, axis, up)
        after = lax.ppermute(first, axis, down)
        x = jnp.concatenate([before, x, after], axis=dim)
    return x


def local(charges, near_blocks, near_src, far_v, far_u, far_rank, far_col, far_row):
    clusters_here = charges.shape[0]
    rhs_count = charges.shape[1]
    elements = charges.shape[2]
    width = far_v.shape[3]
    col_count = lax.axis_size("col")
    row_count = lax.axis_size("row")
    col_here = lax.axis_index("col")
    device_count = row_count * col_count
    slots = far_v.shape[2]
    sources = with_halo(charges, (("col", 0),), clusters_here)
    source_col = near_src // clusters_here % col_count
    position = (
        source_col - col_here + 1 + col_count
    ) % col_count * clusters_here + near_src % clusters_here
    picked = jnp.take(sources, position.reshape(-1), axis=0)
    picked = picked.reshape(clusters_here, near_src.shape[1], rhs_count, elements)
    near = jnp.einsum("lnsa,lnab->lsb", picked, near_blocks, preferred_element_type=jnp.float32)
    selected = jnp.take(charges, far_col[0].reshape(-1), axis=0)
    selected = selected.reshape(device_count, slots, rhs_count, elements)
    proj = jnp.einsum("ecsm,ecrm->ecsr", selected, far_v[0], preferred_element_type=jnp.float32)
    columns = jnp.arange(width, dtype=jnp.int32)
    keep = (columns[None, None, :] < far_rank[0][:, :, None]).astype(jnp.float32)
    coef = (proj * keep[:, :, None, :]).astype(jnp.bfloat16)
    outgoing = coef.reshape(device_count, slots, rhs_count * width)
    incoming = lax.all_to_all(outgoing, ("row", "col"), split_axis=0, concat_axis=0, tiled=True)
    incoming = incoming.reshape(device_count, slots, rhs_count, width)
    locals_here = jnp.arange(clusters_here, dtype=jnp.int32)
    onehot = (far_row[0][:, :, None] == locals_here[None, None, :]).astype(jnp.bfloat16)
    spread = incoming[:, :, None, :, :] * onehot[:, :, :, None, None]
    far = jnp.einsum("dclsr,dcrm->lsm", spread, far_u[0], preferred_element_type=jnp.float32)
    return near + far


def solution(mesh):
    return jax.shard_map(
        local,
        mesh=mesh,
        in_specs=(
            P(("row", "col"), None, None),
            P(("row", "col"), None, None, None),
            P(("row", "col"), None),
            P(("row", "col"), None, None, None, None),
            P(("row", "col"), None, None, None, None),
            P(("row", "col"), None, None),
            P(("row", "col"), None, None),
            P(("row", "col"), None, None),
        ),
        out_specs=P(("row", "col"), None, None),
        check_vma=False,
    )
```

profile of v0, /device:TPU:0, one launch (start us, length us, event | category | flops | bytes accessed | tf_op | source)
XLA Modules:
  0.0 57.4 jit_solution(11558095262912303177)
XLA Ops:
  0.0 3.4 %collective-permute-start.1 = (bf16[2,48,1024]{2,1,0:T(8,128)(2,1)}, bf16[2,48,1024]{2,1,0:T(8,128)(2,1)S(1)}, u32[]{:S(2)}, u32[]{:S(2)}) collective-permute-start(bf16[2,48,1024]{2,1,0:T(8,128)(2,1)} %param.8), channel_id=1, source_target_pairs={{1,0},{2,1},{3,2},{4,3},{5,4},{6,5},{7,6},{0,7},{9,8},{10,9},{11,1... | collective-permute-start | bytes 589832 | tf_op jit(solution)/shard_map/ppermute | solution.py:15
  3.4 0.0 collective-permute-start
  3.4 0.8 %copy.20 = s32[1,32,4]{2,1,0:T(8,128)S(1)} copy(s32[1,32,4]{1,2,0:T(4,128)} %param.14) | data formatting | bytes 1024 | tf_op args[6]
  4.1 0.7 %compare_and_fusion = pred[32,4]{0,1:T(4,128)(4,1)S(1)} fusion(s32[1,32,4]{1,2,0:T(4,128)} %param.14), kind=kLoop, calls=%fused_computation.33 | loop fusion | flops 768 | bytes 640 | tf_op jit(solution)/shard_map/jit(_take)/and | solution.py:38
  4.8 0.1 reshape_squeeze.6
  4.9 0.0 copy-start.1
  5.0 9.1 %gather_fusion.1 = bf16[128,48,1024]{2,1,0:T(8,128)(2,1)} fusion(bf16[2,48,1024]{2,1,0:T(8,128)(2,1)} %param.8, s32[1024]{0:T(1024)S(1)} %pad_clamp_fusion), kind=kCustom, calls=%fused_computation.1 | custom fusion | bytes 25166336 | tf_op jit(solution)/shard_map/jit(_take)/gather | solution.py:38
  14.0 0.1 copy.19
  14.1 0.0 copy-done.1
  14.1 0.1 copy.21
  14.2 0.1 fusion.23
  14.3 0.0 copy-start.3
  14.3 0.0 copy-start.2
  14.3 0.0 copy-start
  14.3 8.9 %multiply_convert_fusion = bf16[32,4,48,32]{2,3,1,0:T(8,128)(2,1)S(1)} fusion(bf16[1,32,4,32,1024]{4,3,2,1,0:T(8,128)(2,1)} %param.11, bf16[32,4,48,1024]{3,2,1,0:T(8,128)(2,1)} %bitcast.35, pred[32,4]{1,0:T(8,128)(4,1)S(1)} %copy.19, f32[32,4,32]{2,1,0:T(4,128)S(1)} %fusion.23), kind=kOutput, calls=%fused_computation.10 | convolution fusion | flops 409337856 | bytes 21381248 | tf_op jit(solution)/shard_map/ecsm,ecrm->ecsr/dot_general | solution.py:40
  23.2 0.8 %copy.30 = bf16[32,4,48,32]{3,2,1,0:T(8,128)(2,1)S(1)} copy(bf16[32,4,48,32]{2,3,1,0:T(8,128)(2,1)S(1)} %multiply_convert_fusion) | data formatting | bytes 786432 | tf_op jit(solution)/shard_map/reshape | solution.py:44
  24.1 1.8 %reshape.113 = bf16[32,4,1536]{2,1,0:T(4,128)(2,1)} reshape(bf16[32,4,48,32]{3,2,1,0:T(8,128)(2,1)S(1)} %copy.30) | data formatting | bytes 786432 | tf_op jit(solution)/shard_map/reshape | solution.py:44
  25.9 6.1 %all-to-all-start = ((bf16[32,4,1536]{2,1,0:T(4,128)(2,1)}), bf16[32,4,1536]{2,1,0:T(4,128)(2,1)S(1)}, u32[]{:S(2)}, u32[]{:S(2)}) async-start(bf16[32,4,1536]{2,1,0:T(4,128)(2,1)} %reshape.113), calls=%async_computation | async-start | bytes 786432 | tf_op jit(solution)/shard_map/all_to_all | solution.py:45
  32.0 0.0 copy-done.3
  32.0 0.1 reshape.92
  32.1 0.0 copy-done.2
  32.1 0.0 collective-permute-done.1
  32.1 0.0 collective-permute-done
  32.2 0.0 copy-done
  32.2 0.1 pad_maximum_fusion
  32.2 0.6 gather_fusion
  32.8 12.4 %all-to-all-done = bf16[32,4,1536]{2,1,0:T(4,128)(2,1)S(1)} async-done(((bf16[32,4,1536]{2,1,0:T(4,128)(2,1)}), bf16[32,4,1536]{2,1,0:T(4,128)(2,1)S(1)}, u32[]{:S(2)}, u32[]{:S(2)}) %all-to-all-start) | async-done | bytes 393248 | tf_op jit(solution)/shard_map/all_to_all | solution.py:45
  45.2 0.9 %reshape.114 = bf16[32,4,48,32]{3,2,1,0:T(8,128)(2,1)S(1)} reshape(bf16[32,4,1536]{2,1,0:T(4,128)(2,1)S(1)} %all-to-all-done) | data formatting | bytes 786432 | tf_op jit(solution)/shard_map/mul | solution.py:49
  46.1 0.8 %copy.25 = bf16[32,4,48,32]{2,3,0,1:T(8,128)(2,1)S(1)} copy(bf16[32,4,48,32]{3,2,1,0:T(8,128)(2,1)S(1)} %reshape.114) | data formatting | bytes 786432 | tf_op jit(solution)/shard_map/mul | solution.py:49
  46.9 4.8 %fusion.13 = f32[2,48,1024]{2,1,0:T(8,128)S(1)} fusion(bf16[32,4,2]{0,2,1:T(2,128)(2,1)S(1)} %compare_convert_fusion, bf16[32,4,48,32]{2,3,0,1:T(8,128)(2,1)S(1)} %copy.25, bf16[1,32,4,32,1024]{4,3,2,1,0:T(8,128)(2,1)} %param.12), kind=kOutput, calls=%fused_computation.13 | convolution fusion | flops 805699584 | bytes 9175552 | tf_op jit(solution)/shard_map/dclsr,dcrm->lsm/dot_general | solution.py:50
  51.7 5.8 %fusion.12 = f32[2,48,1024]{2,1,0:T(8,128)} fusion(f32[2,48,1024]{2,1,0:T(8,128)S(1)} %fusion.13, bf16[2,2,1024,1024]{3,2,1,0:T(8,128)(2,1)} %param.9, bf16[2,2,48,1024]{3,2,1,0:T(8,128)(2,1)S(1)} %bitcast.36, pred[2,2]{1,0:T(4,128)(4,1)S(1)} %get-tuple-element.5), kind=kOutput, calls=%fused_computation.12 | convolution fusion | flops 402948096 | bytes 9568260 | tf_op jit(solution)/shard_map/lnsa,lnab->lsb/dot_general | solution.py:37
  (6 shorter events, 0.1 us)
Async XLA Ops:
  0.0 32.1 %collective-permute-start.1 = (bf16[2,48,1024]{2,1,0:T(8,128)(2,1)}, bf16[2,48,1024]{2,1,0:T(8,128)(2,1)S(1)}, u32[]{:S(2)}, u32[]{:S(2)}) collective-permute-start(bf16[2,48,1024]{2,1,0:T(8,128)(2,1)} %param.8), channel_id=1, source_target_pairs={{1,0},{2,1},{3,2},{4,3},{5,4},{6,5},{7,6},{0,7},{9,8},{10,9},{11,1... | collective-permute-start | bytes 589832 | tf_op jit(solution)/shard_map/ppermute | solution.py:15
  3.4 28.8 %collective-permute-start = (bf16[2,48,1024]{2,1,0:T(8,128)(2,1)}, bf16[2,48,1024]{2,1,0:T(8,128)(2,1)S(1)}, u32[]{:S(2)}, u32[]{:S(2)}) collective-permute-start(bf16[2,48,1024]{2,1,0:T(8,128)(2,1)} %param.8), channel_id=1, source_target_pairs={{0,1},{1,2},{2,3},{3,4},{4,5},{5,6},{6,7},{7,0},{8,9},{9,10},{10,1... | collective-permute-start | bytes 589832 | tf_op jit(solution)/shard_map/ppermute | solution.py:14
  4.9 9.2 %copy-start.1 = (s32[1,32,4]{1,2,0:T(4,128)S(1)}, s32[1,32,4]{1,2,0:T(4,128)}, u32[]{:S(2)}) copy-start(s32[1,32,4]{1,2,0:T(4,128)} %param.13) | copy-start | bytes 1540
  14.3 17.7 %copy-start.3 = (s32[2,2]{1,0:T(2,128)S(1)}, s32[2,2]{1,0:T(2,128)}, u32[]{:S(2)}) copy-start(s32[2,2]{1,0:T(2,128)} %param.10) | copy-start | bytes 52
  14.3 17.8 %copy-start.2 = (s32[1,32,4]{1,2,0:T(4,128)S(1)}, s32[1,32,4]{1,2,0:T(4,128)}, u32[]{:S(2)}) copy-start(s32[1,32,4]{1,2,0:T(4,128)} %param.15) | copy-start | bytes 1540
  14.3 17.8 %copy-start = (bf16[2,48,1024]{2,1,0:T(8,128)(2,1)S(1)}, bf16[2,48,1024]{2,1,0:T(8,128)(2,1)}, u32[]{:S(2)}) copy-start(bf16[2,48,1024]{2,1,0:T(8,128)(2,1)} %param.8) | copy-start | bytes 589828
  25.9 19.3 %all-to-all-start = ((bf16[32,4,1536]{2,1,0:T(4,128)(2,1)}), bf16[32,4,1536]{2,1,0:T(4,128)(2,1)S(1)}, u32[]{:S(2)}, u32[]{:S(2)}) async-start(bf16[32,4,1536]{2,1,0:T(4,128)(2,1)} %reshape.113), calls=%async_computation | async-start | bytes 786432 | tf_op jit(solution)/shard_map/all_to_all | solution.py:45
where the time goes:
time: 57.7 us; the launch traced here: 57.4 us
  matrix products  19.4 us (34%)
  local copies, waits for them, and re-layouts  15.1 us (26%)
  waiting for transfers between devices  12.4 us (21%)
  starting transfers between devices  9.42 us (16%)
  other arithmetic  0.92 us (2%)
    all_to_all x1, waiting for transfers between devices, local(): lax.all_to_all(outgoing, ('row', 'col'), split_axis=0, concat_axis=0, til...  12.4 us
    gather x1, local copies, waits for them, and re-layouts, local(): selected = jnp.take(charges, far_col[0].reshape(-1), axis=0)  9.05 us
    dot_general x1, matrix products, local(): jnp.einsum('ecsm,ecrm->ecsr', selected, far_v[0], preferred_element_type=...  8.88 us
    all_to_all x1, starting transfers between devices, local(): lax.all_to_all(outgoing, ('row', 'col'), split_axis=0, concat_axis=0, til...  6.06 us
    dot_general x1, matrix products, local(): jnp.einsum('lnsa,lnab->lsb', picked, near_blocks, preferred_element_type=...  5.75 us
    dot_general x1, matrix products, local(): jnp.einsum('dclsr,dcrm->lsm', spread, far_u[0], preferred_element_type=jn...  4.77 us
    ppermute x1, starting transfers between devices, with_halo(): after = lax.ppermute(first, axis, down)  3.36 us
    reshape x2, local copies, waits for them, and re-layouts, local(): outgoing = coef.reshape(device_count, slots, rhs_count * width)  2.66 us
  transfers between devices with their start and end apart: 3, of which 1 were waited for; matrix products, arithmetic and copies ran while one was open for 40% of the time, Pallas kernels for 0%

commit v1 on v0

v1 whole, which is shorter than its diff:
```python
import functools

import jax
import jax.numpy as jnp
from jax import lax
from jax.experimental import pallas as pl
from jax.experimental.pallas import tpu as pltpu
from jax.sharding import PartitionSpec as P

MESH = pl.DeviceIdType.MESH
CHUNK_LANES = 512


def kernel(
    rows, cols, group,
    nsrc, ch_hbm, nb_hbm, fv_hbm, fu_hbm, rank_hbm, col_hbm, row_hbm,
    out,
    src, nb, fv, fu, small, spread, send, recv,
    src_sem, nb_sem, fv_sem, fu_sem, small_sem, halo_send, halo_recv, far_send, far_recv,
):
    devices = rows * cols
    clusters, rhs, elements = src.shape[1:]
    slots, width = fv_hbm.shape[2:4]
    lanes = slots * width
    chunks = devices // group
    row_here, col_here = lax.axis_index("row"), lax.axis_index("col")
    me = row_here * cols + col_here
    chunk_here = me // group

    def place(device):
        return (device // cols, device % cols)

    own_copy = pltpu.make_async_copy(ch_hbm, src.at[1], src_sem)
    own_copy.start()
    small_copies = [
        pltpu.make_async_copy(ref, small.at[pl.ds(i, 1)], small_sem.at[i])
        for i, ref in enumerate((rank_hbm, col_hbm, row_hbm))
    ]
    for copy in small_copies:
        copy.start()

    def fv_copy(g):
        chunk = (chunk_here + g) % chunks
        return pltpu.make_async_copy(fv_hbm.at[0, pl.ds(chunk * group, group)], fv.at[g], fv_sem.at[g])

    def fu_copy(g):
        chunk = (chunk_here - g + chunks) % chunks
        return pltpu.make_async_copy(fu_hbm.at[0, pl.ds(chunk * group, group)], fu.at[g], fu_sem.at[g])

    def nb_copy(l, n):
        return pltpu.make_async_copy(nb_hbm.at[l, n], nb.at[l, n], nb_sem.at[l, n])

    near = nb_hbm.shape[1]
    for g in range(chunks):
        fv_copy(g).start()

    barrier = pltpu.get_barrier_semaphore()

    @pl.loop(1, devices)
    def _(step):
        pl.semaphore_signal(barrier, inc=1, device_id=place((me + step) % devices), device_id_type=MESH)

    for l in range(clusters):
        for n in range(near):
            nb_copy(l, n).start()
    for g in range(chunks):
        fu_copy(g).start()

    for copy in small_copies:
        copy.wait()
    for i in range(3):
        table = small[i]
        tall = [jnp.broadcast_to(table[c : c + 1], (width, devices)) for c in range(slots)]
        spread[i] = jnp.concatenate(tall, axis=0).T

    own_copy.wait()
    right = (row_here, (col_here + 1) % cols)
    left = (row_here, (col_here + cols - 1) % cols)
    halos = [
        pltpu.make_async_remote_copy(
            src.at[1], src.at[slot], halo_send.at[i], halo_recv.at[i], device_id=where, device_id_type=MESH
        )
        for i, (slot, where) in enumerate(((0, right), (2, left)))
    ]
    column = lax.broadcasted_iota(jnp.int32, (1, lanes), 1) % width

    def project(g):
        fv_copy(g).wait()
        chunk = (chunk_here + g) % chunks
        mine = src[1].reshape(clusters * rhs, elements)
        factors = fv[g].reshape(group * lanes, elements)
        proj = lax.dot_general(mine, factors, (((1,), (1,)), ((), ())), preferred_element_type=jnp.float32)
        for j in range(group):
            e = chunk * group + j
            part = proj[:, j * lanes : (j + 1) * lanes]
            pick = spread[1, pl.ds(e, 1), :]
            chosen = part[:rhs]
            for l in range(1, clusters):
                chosen = jnp.where(pick == l, part[l * rhs : (l + 1) * rhs], chosen)
            keep = column < spread[0, pl.ds(e, 1), :]
            send[e] = jnp.where(keep, chosen, 0.0).astype(jnp.bfloat16)

    def far_copy(e, source):
        return pltpu.make_async_remote_copy(
            send.at[e], recv.at[source], far_send.at[e], far_recv.at[source], device_id=place(e), device_id_type=MESH
        )

    def post(g):
        chunk = (chunk_here + g) % chunks

        @pl.loop(0, group)
        def _(j):
            e = chunk * group + j

            @pl.when(e != me)
            def _():
                far_copy(e, me).start()

    project(0)
    pl.semaphore_wait(barrier, devices - 1)
    for copy in halos:
        copy.start()

    @pl.loop(1, chunks)
    def _(g):
        project(g)
        post(g - 1)

    recv[me] = send[me]
    out[...] = jnp.zeros_like(out)
    post(chunks - 1)

    for copy in halos:
        copy.wait_recv()
    for l in range(clusters):
        for n in range(near):
            index = nsrc[l, n]
            source_col = index // clusters % cols
            slot = jnp.minimum((source_col - col_here + 1 + cols) % cols, 2)
            picked = src[slot, index % clusters]
            nb_copy(l, n).wait()
            out[l] += jnp.dot(picked, nb[l, n], preferred_element_type=jnp.float32)

    @pl.loop(0, chunks)
    def _(g):
        chunk = (chunk_here - g + chunks) % chunks

        @pl.loop(0, group)
        def _(j):
            d = chunk * group + j

            @pl.when(d != me)
            def _():
                far_copy(d, d).wait_recv()

        fu_copy(g).wait()
        parts = [[] for _ in range(clusters)]
        for j in range(group):
            d = chunk * group + j
            incoming = recv[d].astype(jnp.float32)
            target = spread[2, pl.ds(d, 1), :]
            for l in range(clusters):
                parts[l].append(jnp.where(target == l, incoming, 0.0).astype(jnp.bfloat16))
        left_side = jnp.concatenate([jnp.concatenate(p, axis=1) for p in parts], axis=0)
        factors = fu[g].reshape(group * lanes, elements)
        product = jnp.dot(left_side, factors, preferred_element_type=jnp.float32)
        out[...] += product.reshape(out.shape)

    for copy in halos:
        copy.wait_send()

    @pl.loop(1, devices)
    def _(step):
        far_copy((me + step) % devices, me).wait_send()


def local(charges, near_blocks, near_src, far_v, far_u, far_rank, far_col, far_row):
    cols = lax.axis_size("col")
    rows = lax.axis_size("row")
    devices = rows * cols
    clusters, rhs, elements = charges.shape
    near = near_blocks.shape[1]
    slots, width = far_v.shape[2:4]
    lanes = slots * width
    group = max(1, min(devices, CHUNK_LANES // lanes))
    while devices % group:
        group -= 1
    chunks = devices // group
    anywhere = pl.BlockSpec(memory_space=pl.ANY)
    factors = (chunks, group, slots, width, elements)
    tables = [jnp.swapaxes(table, 1, 2) for table in (far_rank, far_col, far_row)]
    return pl.pallas_call(
        functools.partial(kernel, rows, cols, group),
        out_shape=pltpu.VMEM((clusters, rhs, elements), jnp.float32),
        in_specs=[pl.BlockSpec(memory_space=pltpu.SMEM)] + [anywhere] * 7,
        out_specs=pl.BlockSpec(memory_space=pltpu.VMEM),
        scratch_shapes=[
            pltpu.VMEM((3, clusters, rhs, elements), jnp.bfloat16),
            pltpu.VMEM(near_blocks.shape, jnp.bfloat16),
            pltpu.VMEM(factors, jnp.bfloat16),
            pltpu.VMEM(factors, jnp.bfloat16),
            pltpu.VMEM((3, slots, devices), jnp.int32),
            pltpu.VMEM((3, devices, lanes), jnp.int32),
            pltpu.VMEM((devices, rhs, lanes), jnp.bfloat16),
            pltpu.VMEM((devices, rhs, lanes), jnp.bfloat16),
            pltpu.SemaphoreType.DMA,
            pltpu.SemaphoreType.DMA((clusters, near)),
            pltpu.SemaphoreType.DMA((chunks,)),
            pltpu.SemaphoreType.DMA((chunks,)),
            pltpu.SemaphoreType.DMA((3,)),
            pltpu.SemaphoreType.DMA((2,)),
            pltpu.SemaphoreType.DMA((2,)),
            pltpu.SemaphoreType.DMA((devices,)),
            pltpu.SemaphoreType.DMA((devices,)),
        ],
        compiler_params=pltpu.CompilerParams(
            collective_id=0, has_side_effects=True, vmem_limit_bytes=60 * 1024 * 1024
        ),
    )(near_src, charges, near_blocks, far_v, far_u, *tables)


def solution(mesh):
    return jax.shard_map(
        local,
        mesh=mesh,
        in_specs=(
            P(("row", "col"), None, None),
            P(("row", "col"), None, None, None),
            P(("row", "col"), None),
            P(("row", "col"), None, None, None, None),
            P(("row", "col"), None, None, None, None),
            P(("row", "col"), None, None),
            P(("row", "col"), None, None),
            P(("row", "col"), None, None),
        ),
        out_specs=P(("row", "col"), None, None),
        check_vma=False,
    )
```

time: 57.7 us -> 21.9 us (0.38)
  the two profiles are of different devices: /device:TPU:0 before, /device:TPU:1 now
where the time goes in v1:
time: 21.9 us; the launch traced here: 21.7 us
  Pallas kernels  21 us (96%)
  local copies, waits for them, and re-layouts  0.75 us (3%)
    pallas_call x1, Pallas kernels, local(): pl.pallas_call(functools.partial(kernel, rows, cols, group), out_shape=pl...  21 us
    unnamed x1, local copies, waits for them, and re-layouts  0.75 us

profile of v1, /device:TPU:1, one launch (start us, length us, event | category | flops | bytes accessed | tf_op | source)
XLA Modules:
  0.0 21.7 jit_solution(4742624682025030586)
XLA Ops:
  0.0 21.0 %shard_map.82 = f32[2,48,1024]{2,1,0:T(8,128)S(1)} custom-call(s32[2,2]{1,0:T(2,128)} %nsrc.1, bf16[2,48,1024]{2,1,0:T(8,128)(2,1)} %ch_hbm.1, bf16[2,2,1024,1024]{3,2,1,0:T(8,128)(2,1)} %nb_hbm.1, bf16[1,32,4,32,1024]{4,3,2,1,0:T(8,128)(2,1)} %fv_hbm.1, bf16[1,32,4,32,1024]{4,3,2,1,0:T(8,128)(2,1)} %fu_hbm.1, s32[1,4,32]{2,1,0:T(4,128)} %bitcast.3, ...), custom_call_target="tpu_custom_call" | custom-call | tf_op jit(solution)/shard_map/pallas_call | solution.py:192
  21.0 0.7 %copy.10 = f32[2,48,1024]{2,1,0:T(8,128)} copy(f32[2,48,1024]{2,1,0:T(8,128)S(1)} %shard_map.82) | data formatting | bytes 786432

commit v2 on v1

--- a/solution.py
+++ b/solution.py
@@ -141,7 +141,7 @@
             nb_copy(l, n).wait()
             out[l] += jnp.dot(picked, nb[l, n], preferred_element_type=jnp.float32)
 
-    @pl.loop(0, chunks)
+    @pl.loop(0, chunks, unroll=True)
     def _(g):
         chunk = (chunk_here - g + chunks) % chunks
 

time: 21.9 us -> 20.8 us (0.950)
  Pallas kernels: 21 us -> 19.9 us
    pallas_call x1, Pallas kernels: 21 us -> 19.9 us  [local(): pl.pallas_call(functools.partial(kernel, rows, cols, group), out_shape=pl...]
where the time goes in v2:
time: 20.8 us; the launch traced here: 20.6 us
  Pallas kernels  19.9 us (96%)
  local copies, waits for them, and re-layouts  0.75 us (4%)
    pallas_call x1, Pallas kernels, local(): pl.pallas_call(functools.partial(kernel, rows, cols, group), out_shape=pl...  19.9 us
    unnamed x1, local copies, waits for them, and re-layouts  0.75 us

profile of v2, /device:TPU:1, one launch (start us, length us, event | category | flops | bytes accessed | tf_op | source)
XLA Modules:
  0.0 20.6 jit_solution(642836704281454401)
XLA Ops:
  0.0 19.9 %shard_map.82 = f32[2,48,1024]{2,1,0:T(8,128)S(1)} custom-call(s32[2,2]{1,0:T(2,128)} %nsrc.1, bf16[2,48,1024]{2,1,0:T(8,128)(2,1)} %ch_hbm.1, bf16[2,2,1024,1024]{3,2,1,0:T(8,128)(2,1)} %nb_hbm.1, bf16[1,32,4,32,1024]{4,3,2,1,0:T(8,128)(2,1)} %fv_hbm.1, bf16[1,32,4,32,1024]{4,3,2,1,0:T(8,128)(2,1)} %fu_hbm.1, s32[1,4,32]{2,1,0:T(4,128)} %bitcast.3, ...), custom_call_target="tpu_custom_call" | custom-call | tf_op jit(solution)/shard_map/pallas_call | solution.py:192
  19.9 0.7 %copy.10 = f32[2,48,1024]{2,1,0:T(8,128)} copy(f32[2,48,1024]{2,1,0:T(8,128)S(1)} %shard_map.82) | data formatting | bytes 786432
